TPU v7x, 512 devices: a whole 4x4x16 slice. The times are simulated.
512 devices in a mesh: row: 16 (over z), col: 8 (over x_lo, y), depth: 4 (over x_hi, core).
Axes of the slice: x: 4 (x_hi: 2, x_lo: 2; x = x_hi * 2 + x_lo), y: 4, z: 16, core: 2. Of those that a mesh axis runs over, the one named last changes fastest.
Arguments:
- h_blocks: bfloat16 [16, 16, 4, 12, 128, 128], P('row', 'col', 'depth'), may hold values from -0.25 to 0.25
- h_rows: int32 [16, 16, 4, 12], P('row', 'col', 'depth'), may hold values from 0 to 31, as said below
- h_cols: int32 [16, 16, 4, 12], P('row', 'col', 'depth'), may hold values from 0 to 7
- h_flags: int32 [16, 16, 4, 12], P('row', 'col', 'depth'), may hold values from 0 to 1
- x_blocks: bfloat16 [16, 4, 8, 8, 2, 128, 128], P('row', 'depth', 'col'), may hold values from -6 to 6
- x_cols: int32 [16, 4, 8, 8, 2], P('row', 'depth', 'col'), may hold values from 0 to 7, as said below
- x_flags: int32 [16, 4, 8, 8, 2], P('row', 'depth', 'col'), may hold values from 0 to 1
- previous: bfloat16 [16, 4, 8, 8, 2, 128, 128], P('row', 'depth', 'col'), may hold values from -6 to 6
Outputs:
- next_term: bfloat16 [16, 4, 8, 8, 2, 128, 128], P('row', 'depth', 'col')
Inputs may be any that keep to these rules, and one draw needn't show every extreme that they name: The slots of one tile (g, p, e) name distinct positions (h_rows, h_cols); live slots come first; every tile with g = p has all 12 slots live. `x_cols`: the 2 slots of one block row in one column group name distinct columns.
All inputs are finite; a program needn't handle non-finite values.
Results may differ from a plain program's by a relative error of at most 0.0095.
Values may be sent and summed in bfloat16 or wider, within the bound.
No kernel may reach another device: no remote copies, remote signals or barrier semaphores. Data moves between devices by JAX's collectives and lax.ppermute only.
A program may use at most 64 MiB of HBM per device.

v0:
```python
import jax
import jax.numpy as jnp
from jax import lax
from jax.sharding import PartitionSpec as P


def add_piece(summed, ham_part, iter_part, aim_cols, aim_flags):
    blocks, ham_rows, ham_cols, ham_flags = ham_part
    iter_blocks, iter_cols, iter_flags = iter_part
    iter_width = iter_cols.shape[-1]
    picked = jnp.take(iter_blocks, ham_cols, axis=0)
    picked_cols = jnp.take(iter_cols, ham_cols, axis=0)
    picked_flags = jnp.take(iter_flags, ham_cols, axis=0)
    wanted_cols = jnp.take(aim_cols, ham_rows, axis=0)
    wanted_flags = jnp.take(aim_flags, ham_rows, axis=0)
    paired = picked_cols[:, :, None] == wanted_cols[:, None, :]
    paired = paired & (picked_flags[:, :, None] > 0) & (wanted_flags[:, None, :] > 0)
    paired = paired & (ham_flags[:, None, None] > 0)
    chosen = jnp.einsum(
        "awv,awkm->avkm", paired.astype(jnp.bfloat16), picked, preferred_element_type=jnp.float32
    ).astype(jnp.bfloat16)
    products = jnp.einsum("akl,avlm->avkm", blocks, chosen, preferred_element_type=jnp.float32)
    target = ham_rows[:, None] * iter_width + jnp.arange(iter_width, dtype=jnp.int32)[None, :]
    return summed.at[target.reshape(-1)].add(products.reshape((-1,) + products.shape[2:]))


def run_pieces(summed, ham_part, iter_part, aim_cols, aim_flags):

    def one_piece(running, element):
        ham_item, iter_item = element
        running = add_piece(running, ham_item, iter_item, aim_cols, aim_flags)
        return (running, None)

    summed, _ = lax.scan(one_piece, summed, (ham_part, iter_part))
    return summed


def body(h_blocks, h_rows, h_cols, h_flags, x_blocks, x_cols, x_flags, previous):
    aim_cols, aim_flags = (
        lax.all_gather(x_cols, "depth", axis=1, tiled=True),
        lax.all_gather(x_flags, "depth", axis=1, tiled=True),
    )
    iter_width = x_cols.shape[-1]
    piece_rows = x_cols.shape[3]
    block_size = x_blocks.shape[-1]
    aim_cols = aim_cols.reshape(-1, iter_width)
    aim_flags = aim_flags.reshape(-1, iter_width)
    group_rows = aim_cols.shape[0]
    summed = jnp.zeros((group_rows * iter_width, block_size, block_size), jnp.float32)
    ham_all = (
        lax.all_gather(h_blocks, "col", axis=1, tiled=True),
        lax.all_gather(h_rows, "col", axis=1, tiled=True),
        lax.all_gather(h_cols, "col", axis=1, tiled=True),
        lax.all_gather(h_flags, "col", axis=1, tiled=True),
    )
    ham_all = tuple((member[0, :, 0] for member in ham_all))
    pieces = (
        lax.all_gather(x_blocks, "row", axis=0, tiled=True),
        lax.all_gather(x_cols, "row", axis=0, tiled=True),
        lax.all_gather(x_flags, "row", axis=0, tiled=True),
    )
    ham_part = tuple((member for member in ham_all))
    iter_part = tuple((member[:, 0, 0] for member in pieces))
    summed = run_pieces(summed, ham_part, iter_part, aim_cols, aim_flags)
    rounded = lax.optimization_barrier(summed.astype(jnp.bfloat16)).astype(jnp.float32)
    rounded = rounded.reshape(
        (lax.axis_size("depth"), piece_rows, iter_width, block_size, block_size)
    )
    shares = lax.psum_scatter(
        rounded.astype(jnp.bfloat16), "depth", scatter_dimension=0, tiled=True
    ).astype(jnp.float32)
    prior = previous[0, 0, 0].astype(jnp.float32)
    live = x_flags[0, 0, 0].astype(jnp.float32)[..., None, None]
    result = (2.0 * shares[0] - prior) * live
    return result.astype(jnp.bfloat16).reshape(previous.shape)


def solution(mesh):
    placed = (
        P("row", "col", "depth", None, None, None),
        P("row", "col", "depth", None),
        P("row", "col", "depth", None),
        P("row", "col", "depth", None),
        P("row", "depth", "col", None, None, None, None),
        P("row", "depth", "col", None, None),
        P("row", "depth", "col", None, None),
        P("row", "depth", "col", None, None, None, None),
    )
    return jax.shard_map(
        body,
        mesh=mesh,
        in_specs=placed,
        out_specs=P("row", "depth", "col", None, None, None, None),
        check_vma=False,
    )
```

profile of v0, /device:TPU:1, one launch (start us, length us, event | category | flops | bytes accessed | tf_op | source)
XLA Modules:
  0.0 491.7 jit_solution(9868348673197642162)
XLA Ops:
  8.1 13.5 %all_gather.30 = s32[1,4,1,8,2]{3,4,2,0,1:T(2,128)S(1)} all-gather(s32[1,1,1,8,2]{3,4,2,0,1:T(2,128)} %bitcast.95), channel_id=1, replica_groups=mesh['row'=16,'col'=8,'depth'=4] {'depth'}, dimensions={1}, use_global_device_ids=true | all-gather | bytes 320 | tf_op jit(solution)/shard_map/all_gather | solution.py:40
  21.6 6.8 %all_gather.32 = s32[1,4,1,8,2]{3,4,2,0,1:T(2,128)S(1)} all-gather(s32[1,1,1,8,2]{3,4,2,0,1:T(2,128)} %bitcast.93), channel_id=1, replica_groups=mesh['row'=16,'col'=8,'depth'=4] {'depth'}, dimensions={1}, use_global_device_ids=true | all-gather | bytes 320 | tf_op jit(solution)/shard_map/all_gather | solution.py:41
  28.5 12.7 %all_gather.27 = s32[1,16,1,12]{3,2,0,1:T(1,128)S(1)} all-gather(s32[1,2,1,12]{3,2,0,1:T(1,128)} %bitcast.96), channel_id=1, replica_groups=mesh['row'=16,'col'=8,'depth'=4] {'col'}, dimensions={1}, use_global_device_ids=true | all-gather | bytes 864 | tf_op jit(solution)/shard_map/all_gather | solution.py:52
  41.2 15.2 %all_gather.29 = s32[1,16,1,12]{3,2,0,1:T(1,128)S(1)} all-gather(s32[1,2,1,12]{3,2,0,1:T(1,128)} %bitcast.97), channel_id=1, replica_groups=mesh['row'=16,'col'=8,'depth'=4] {'col'}, dimensions={1}, use_global_device_ids=true | all-gather | bytes 864 | tf_op jit(solution)/shard_map/all_gather | solution.py:53
  56.4 13.5 %all_gather.33 = s32[1,16,1,12]{3,2,0,1:T(1,128)S(1)} all-gather(s32[1,2,1,12]{3,2,0,1:T(1,128)} %bitcast.98), channel_id=1, replica_groups=mesh['row'=16,'col'=8,'depth'=4] {'col'}, dimensions={1}, use_global_device_ids=true | all-gather | bytes 864 | tf_op jit(solution)/shard_map/all_gather | solution.py:54
  70.0 29.6 %all_gather.28 = s32[16,1,1,8,2]{3,4,2,1,0:T(2,128)S(1)} all-gather(s32[1,1,1,8,2]{3,4,2,1,0:T(2,128)} %param.19), channel_id=1, replica_groups=mesh['row'=16,'col'=8,'depth'=4] {'row'}, dimensions={0}, use_global_device_ids=true | all-gather | bytes 1088 | tf_op jit(solution)/shard_map/all_gather | solution.py:59
  99.5 20.1 %all_gather.31 = s32[16,1,1,8,2]{3,4,2,1,0:T(2,128)S(1)} all-gather(s32[1,1,1,8,2]{3,4,2,1,0:T(2,128)} %param.20), channel_id=1, replica_groups=mesh['row'=16,'col'=8,'depth'=4] {'row'}, dimensions={0}, use_global_device_ids=true | all-gather | bytes 1088 | tf_op jit(solution)/shard_map/all_gather | solution.py:60
  119.6 82.3 %all-gather.3.cloned.1.call-done = bf16[16,1,1,8,2,128,128]{6,5,4,3,2,1,0:T(8,128)(2,1)} async-done(((bf16[1,1,1,8,2,128,128]{6,5,4,3,2,1,0:T(8,128)(2,1)}), bf16[16,1,1,8,2,128,128]{6,5,4,3,2,1,0:T(8,128)(2,1)}) %all-gather.3.cloned.1.call-update) | async-done | bytes 8388624 | tf_op jit(solution)/shard_map/all_gather | solution.py:58
  201.9 2.5 broadcast_in_dim.36
  204.4 223.1 %while.10 = (s32[]{:T(128)}, f32[64,128,128]{2,1,0:T(8,128)}, s32[16,12]{1,0:T(8,128)S(1)}, s32[16,8,2]{1,2,0:T(2,128)S(1)}, s32[16,12]{1,0:T(8,128)S(1)}, /*ind...) while((s32[]{:T(128)}, f32[64,128,128]{2,1,0:T(8,128)}, ...), condition=%wide.region_2.5_spmd, body=%wide.region_0.4_spmd.sunk | while | flops 103419520 | bytes 16400633 | solution.py:34
  205.9 1.1 dynamic-slice_bitcast_fusion.2
  209.1 1.0 convolution_convert_fusion.2
  210.2 1.4 fusion.34
  212.3 6.1 %scatter_fusion = f32[64,128,128]{2,1,0:T(8,128)} fusion(f32[64,128,128]{2,1,0:T(8,128)} %get-tuple-element.231, s32[24]{0:T(128)S(1)} %fusion.31, f32[24,128,128]{2,1,0:T(8,128)S(1)} %copy.89), kind=kCustom, calls=%fused_computation.5.clone.1 | custom fusion | flops 393216 | bytes 4718688 | tf_op jit(solution)/shard_map/while/body/eval_jaxpr/scatter-add | solution.py:24
  219.8 1.1 dynamic-slice_bitcast_fusion.2
  224.1 1.4 fusion.34
  226.2 6.1 %scatter_fusion = f32[64,128,128]{2,1,0:T(8,128)} fusion(f32[64,128,128]{2,1,0:T(8,128)} %get-tuple-element.231, s32[24]{0:T(128)S(1)} %fusion.31, f32[24,128,128]{2,1,0:T(8,128)S(1)} %copy.89), kind=kCustom, calls=%fused_computation.5.clone.1 | custom fusion | flops 393216 | bytes 4718688 | tf_op jit(solution)/shard_map/while/body/eval_jaxpr/scatter-add | solution.py:24
  233.8 1.1 dynamic-slice_bitcast_fusion.2
  238.1 1.4 fusion.34
  240.1 6.2 %scatter_fusion = f32[64,128,128]{2,1,0:T(8,128)} fusion(f32[64,128,128]{2,1,0:T(8,128)} %get-tuple-element.231, s32[24]{0:T(128)S(1)} %fusion.31, f32[24,128,128]{2,1,0:T(8,128)S(1)} %copy.89), kind=kCustom, calls=%fused_computation.5.clone.1 | custom fusion | flops 393216 | bytes 4718688 | tf_op jit(solution)/shard_map/while/body/eval_jaxpr/scatter-add | solution.py:24
  247.8 1.1 dynamic-slice_bitcast_fusion.2
  252.1 1.4 fusion.34
  254.2 6.1 %scatter_fusion = f32[64,128,128]{2,1,0:T(8,128)} fusion(f32[64,128,128]{2,1,0:T(8,128)} %get-tuple-element.231, s32[24]{0:T(128)S(1)} %fusion.31, f32[24,128,128]{2,1,0:T(8,128)S(1)} %copy.89), kind=kCustom, calls=%fused_computation.5.clone.1 | custom fusion | flops 393216 | bytes 4718688 | tf_op jit(solution)/shard_map/while/body/eval_jaxpr/scatter-add | solution.py:24
  261.8 1.1 dynamic-slice_bitcast_fusion.2
  266.1 1.4 fusion.34
  268.2 6.0 %scatter_fusion = f32[64,128,128]{2,1,0:T(8,128)} fusion(f32[64,128,128]{2,1,0:T(8,128)} %get-tuple-element.231, s32[24]{0:T(128)S(1)} %fusion.31, f32[24,128,128]{2,1,0:T(8,128)S(1)} %copy.89), kind=kCustom, calls=%fused_computation.5.clone.1 | custom fusion | flops 393216 | bytes 4718688 | tf_op jit(solution)/shard_map/while/body/eval_jaxpr/scatter-add | solution.py:24
  275.7 1.1 dynamic-slice_bitcast_fusion.2
  280.0 1.4 fusion.34
  282.1 6.1 %scatter_fusion = f32[64,128,128]{2,1,0:T(8,128)} fusion(f32[64,128,128]{2,1,0:T(8,128)} %get-tuple-element.231, s32[24]{0:T(128)S(1)} %fusion.31, f32[24,128,128]{2,1,0:T(8,128)S(1)} %copy.89), kind=kCustom, calls=%fused_computation.5.clone.1 | custom fusion | flops 393216 | bytes 4718688 | tf_op jit(solution)/shard_map/while/body/eval_jaxpr/scatter-add | solution.py:24
  289.7 1.1 dynamic-slice_bitcast_fusion.2
  294.0 1.4 fusion.34
  296.1 6.0 %scatter_fusion = f32[64,128,128]{2,1,0:T(8,128)} fusion(f32[64,128,128]{2,1,0:T(8,128)} %get-tuple-element.231, s32[24]{0:T(128)S(1)} %fusion.31, f32[24,128,128]{2,1,0:T(8,128)S(1)} %copy.89), kind=kCustom, calls=%fused_computation.5.clone.1 | custom fusion | flops 393216 | bytes 4718688 | tf_op jit(solution)/shard_map/while/body/eval_jaxpr/scatter-add | solution.py:24
  303.6 1.1 dynamic-slice_bitcast_fusion.2
  307.9 1.4 fusion.34
  310.0 6.0 %scatter_fusion = f32[64,128,128]{2,1,0:T(8,128)} fusion(f32[64,128,128]{2,1,0:T(8,128)} %get-tuple-element.231, s32[24]{0:T(128)S(1)} %fusion.31, f32[24,128,128]{2,1,0:T(8,128)S(1)} %copy.89), kind=kCustom, calls=%fused_computation.5.clone.1 | custom fusion | flops 393216 | bytes 4718688 | tf_op jit(solution)/shard_map/while/body/eval_jaxpr/scatter-add | solution.py:24
  317.5 1.1 dynamic-slice_bitcast_fusion.2
  321.8 1.4 fusion.34
  323.9 6.0 %scatter_fusion = f32[64,128,128]{2,1,0:T(8,128)} fusion(f32[64,128,128]{2,1,0:T(8,128)} %get-tuple-element.231, s32[24]{0:T(128)S(1)} %fusion.31, f32[24,128,128]{2,1,0:T(8,128)S(1)} %copy.89), kind=kCustom, calls=%fused_computation.5.clone.1 | custom fusion | flops 393216 | bytes 4718688 | tf_op jit(solution)/shard_map/while/body/eval_jaxpr/scatter-add | solution.py:24
  331.4 1.1 dynamic-slice_bitcast_fusion.2
  335.7 1.4 fusion.34
  337.8 6.0 %scatter_fusion = f32[64,128,128]{2,1,0:T(8,128)} fusion(f32[64,128,128]{2,1,0:T(8,128)} %get-tuple-element.231, s32[24]{0:T(128)S(1)} %fusion.31, f32[24,128,128]{2,1,0:T(8,128)S(1)} %copy.89), kind=kCustom, calls=%fused_computation.5.clone.1 | custom fusion | flops 393216 | bytes 4718688 | tf_op jit(solution)/shard_map/while/body/eval_jaxpr/scatter-add | solution.py:24
  345.3 1.1 dynamic-slice_bitcast_fusion.2
  348.6 1.0 convolution_convert_fusion.2
  349.6 1.4 fusion.34
  351.7 6.0 %scatter_fusion = f32[64,128,128]{2,1,0:T(8,128)} fusion(f32[64,128,128]{2,1,0:T(8,128)} %get-tuple-element.231, s32[24]{0:T(128)S(1)} %fusion.31, f32[24,128,128]{2,1,0:T(8,128)S(1)} %copy.89), kind=kCustom, calls=%fused_computation.5.clone.1 | custom fusion | flops 393216 | bytes 4718688 | tf_op jit(solution)/shard_map/while/body/eval_jaxpr/scatter-add | solution.py:24
  359.2 1.1 dynamic-slice_bitcast_fusion.2
  363.5 1.4 fusion.34
  365.6 6.1 %scatter_fusion = f32[64,128,128]{2,1,0:T(8,128)} fusion(f32[64,128,128]{2,1,0:T(8,128)} %get-tuple-element.231, s32[24]{0:T(128)S(1)} %fusion.31, f32[24,128,128]{2,1,0:T(8,128)S(1)} %copy.89), kind=kCustom, calls=%fused_computation.5.clone.1 | custom fusion | flops 393216 | bytes 4718688 | tf_op jit(solution)/shard_map/while/body/eval_jaxpr/scatter-add | solution.py:24
  373.2 1.1 dynamic-slice_bitcast_fusion.2
  377.5 1.4 fusion.34
  379.6 6.1 %scatter_fusion = f32[64,128,128]{2,1,0:T(8,128)} fusion(f32[64,128,128]{2,1,0:T(8,128)} %get-tuple-element.231, s32[24]{0:T(128)S(1)} %fusion.31, f32[24,128,128]{2,1,0:T(8,128)S(1)} %copy.89), kind=kCustom, calls=%fused_computation.5.clone.1 | custom fusion | flops 393216 | bytes 4718688 | tf_op jit(solution)/shard_map/while/body/eval_jaxpr/scatter-add | solution.py:24
  387.1 1.1 dynamic-slice_bitcast_fusion.2
  390.4 1.0 convolution_convert_fusion.2
  391.4 1.4 fusion.34
  393.5 6.1 %scatter_fusion = f32[64,128,128]{2,1,0:T(8,128)} fusion(f32[64,128,128]{2,1,0:T(8,128)} %get-tuple-element.231, s32[24]{0:T(128)S(1)} %fusion.31, f32[24,128,128]{2,1,0:T(8,128)S(1)} %copy.89), kind=kCustom, calls=%fused_computation.5.clone.1 | custom fusion | flops 393216 | bytes 4718688 | tf_op jit(solution)/shard_map/while/body/eval_jaxpr/scatter-add | solution.py:24
  401.1 1.1 dynamic-slice_bitcast_fusion.2
  405.4 1.4 fusion.34
  407.5 6.0 %scatter_fusion = f32[64,128,128]{2,1,0:T(8,128)} fusion(f32[64,128,128]{2,1,0:T(8,128)} %get-tuple-element.231, s32[24]{0:T(128)S(1)} %fusion.31, f32[24,128,128]{2,1,0:T(8,128)S(1)} %copy.89), kind=kCustom, calls=%fused_computation.5.clone.1 | custom fusion | flops 393216 | bytes 4718688 | tf_op jit(solution)/shard_map/while/body/eval_jaxpr/scatter-add | solution.py:24
  415.0 1.1 dynamic-slice_bitcast_fusion.2
  419.3 1.4 fusion.34
  421.4 6.1 %scatter_fusion = f32[64,128,128]{2,1,0:T(8,128)} fusion(f32[64,128,128]{2,1,0:T(8,128)} %get-tuple-element.231, s32[24]{0:T(128)S(1)} %fusion.31, f32[24,128,128]{2,1,0:T(8,128)S(1)} %copy.89), kind=kCustom, calls=%fused_computation.5.clone.1 | custom fusion | flops 393216 | bytes 4718688 | tf_op jit(solution)/shard_map/while/body/eval_jaxpr/scatter-add | solution.py:24
  427.5 4.0 convert_element_type.33
  431.6 51.6 %reduce-scatter.2.cloned.1.call-done = bf16[1,8,2,128,128]{4,3,2,1,0:T(8,128)(2,1)} async-done(((bf16[4,8,2,128,128]{4,3,2,1,0:T(8,128)(2,1)}), bf16[1,8,2,128,128]{4,3,2,1,0:T(8,128)(2,1)}) %reduce-scatter.2.cloned.1.call-update) | async-done | bytes 524304 | tf_op jit(solution)/shard_map/reduce_scatter | solution.py:69
  483.1 2.1 fusion.20
  (412 shorter events, 82.9 us)
Async XLA Ops:
  6.5 113.1 %all-gather.5.cloned.1.call-start = ((), (), s32[]{:S(2)}) async-start(), calls=%async_computation.2 | async-start | bytes 7077888 | tf_op jit(solution)/shard_map/all_gather | solution.py:51
  7.3 194.6 %all-gather.3.cloned.1.call-start = ((), (), s32[]{:S(2)}) async-start(), calls=%async_computation.1 | async-start | bytes 8912896 | tf_op jit(solution)/shard_map/all_gather | solution.py:58
  8.0 475.1 %reduce-scatter.2.cloned.1.call-start = ((), (), s32[]{:S(2)}) async-start(), calls=%async_computation.3 | async-start | bytes 2621440 | tf_op jit(solution)/shard_map/reduce_scatter | solution.py:69
  427.5 4.0 copy-start.1
  427.5 55.7 %copy-start = (bf16[1,1,1,8,2,128,128]{6,5,4,3,2,1,0:T(8,128)(2,1)S(1)}, bf16[1,1,1,8,2,128,128]{6,5,4,3,2,1,0:T(8,128)(2,1)}, u32[]{:S(2)}) copy-start(bf16[1,1,1,8,2,128,128]{6,5,4,3,2,1,0:T(8,128)(2,1)} %param.21) | copy-start | bytes 1572868
Sparse Core Ops, SparseCore 0:
  9.4 85.4 all-gather.4
  97.0 104.8 all-gather.2
  431.6 51.5 reduce-scatter.1
where the time goes:
time: 495 us; the launch traced here: 492 us
  waiting for transfers between devices  135 us (27%)
  other arithmetic  112 us (23%)
  blocking collectives  111 us (22%)
  local copies, waits for them, and re-layouts  78.5 us (16%)
  matrix products  39.2 us (8%)
  between operations  13.1 us (3%)
    scatter-add x16, other arithmetic, add_piece(): summed.at[target.reshape(-1)]  97.1 us
    all_gather x1, waiting for transfers between devices, body(): lax.all_gather(x_blocks, 'row', axis=0, tiled=True)  82.3 us
    reduce_scatter x1, waiting for transfers between devices, body(): lax.psum_scatter(rounded.astype(jnp.bfloat16), 'depth', scatter_dimension...  51.6 us
    all_gather x1, blocking collectives, body(): lax.all_gather(x_cols, 'row', axis=0, tiled=True)  29.6 us
    dot_general x16, matrix products, add_piece(): jnp.einsum('akl,avlm->avkm', blocks, chosen, preferred_element_type=jnp.f...  22.6 us
    all_gather x1, blocking collectives, body(): lax.all_gather(x_flags, 'row', axis=0, tiled=True)  20.1 us
    squeeze x64, local copies, waits for them, and re-layouts, run_pieces(): summed, _ = lax.scan(one_piece, summed, (ham_part, iter_part))  20.1 us
    dot_general x16, matrix products, add_piece(): jnp.einsum('awv,awkm->avkm', paired.astype(jnp.bfloat16), picked, preferr...  16.7 us
  transfers between devices with their start and end apart: 3, of which 2 were waited for; matrix products, arithmetic and copies ran while one was open for 0% of the time, Pallas kernels for 0%

commit v1 on v0

--- a/solution.py
+++ b/solution.py
@@ -2,6 +2,19 @@
 import jax.numpy as jnp
 from jax import lax
 from jax.sharding import PartitionSpec as P
+from jax.lax import all_to_all, axis_size
+
+
+def launch_roots(matrix, dev_axis, on_dim):
+    return jnp.concatenate(
+        all_to_all(
+            jnp.stack(tuple((matrix for _ in range(axis_size(dev_axis)))), axis=0),
+            dev_axis,
+            concat_axis=0,
+            split_axis=0,
+        ),
+        axis=on_dim,
+    )
 
 
 def add_piece(summed, ham_part, iter_part, aim_cols, aim_flags):
@@ -55,7 +68,7 @@
     )
     ham_all = tuple((member[0, :, 0] for member in ham_all))
     pieces = (
-        lax.all_gather(x_blocks, "row", axis=0, tiled=True),
+        launch_roots(x_blocks, "row", 0),
         lax.all_gather(x_cols, "row", axis=0, tiled=True),
         lax.all_gather(x_flags, "row", axis=0, tiled=True),
     )

time: 495 us -> 737 us (1.49)
  blocking collectives: 111 us -> 399 us
  waiting for transfers between devices: 135 us -> 66.2 us
  starting transfers between devices: 0.08 us -> 16 us
    all_gather x1, blocking collectives: 29.6 us -> 320 us  [body(): lax.all_gather(x_cols, 'row', axis=0, tiled=True)]
    all_gather x1 -> x0, waiting for transfers between devices: 82.3 us -> none  [body(): lax.all_gather(x_blocks, 'row', axis=0, tiled=True)]
    all_to_all x0 -> x1, starting transfers between devices: none -> 15.9 us  [launch_roots(): all_to_all(jnp.stack(tuple((matrix for _ in range(axis_size(dev_axis)))),...]
    reduce_scatter x1, waiting for transfers between devices: 51.6 us -> 65.5 us  [body(): lax.psum_scatter(rounded.astype(jnp.bfloat16), 'depth', scatter_dimension...]
  transfers between devices with their start and end apart: 3 -> 3, of which waited for: 2 -> 1; matrix products, arithmetic and copies ran while one was open for 0% -> 0% of each run, Pallas kernels for 0% -> 0%
where the time goes in v1:
time: 737 us; the launch traced here: 733 us
  blocking collectives  399 us (54%)
  other arithmetic  112 us (15%)
  local copies, waits for them, and re-layouts  84.9 us (12%)
  waiting for transfers between devices  66.2 us (9%)
  matrix products  39.2 us (5%)
  starting transfers between devices  16 us (2%)
  between operations  13.5 us (2%)
    all_gather x1, blocking collectives, body(): lax.all_gather(x_cols, 'row', axis=0, tiled=True)  320 us
    scatter-add x16, other arithmetic, add_piece(): summed.at[target.reshape(-1)]  96.6 us
    reduce_scatter x1, waiting for transfers between devices, body(): lax.psum_scatter(rounded.astype(jnp.bfloat16), 'depth', scatter_dimension...  65.5 us
    dot_general x16, matrix products, add_piece(): jnp.einsum('akl,avlm->avkm', blocks, chosen, preferred_element_type=jnp.f...  22.6 us
    all_gather x1, blocking collectives, body(): lax.all_gather(x_flags, 'row', axis=0, tiled=True)  20.4 us
    squeeze x64, local copies, waits for them, and re-layouts, run_pieces(): summed, _ = lax.scan(one_piece, summed, (ham_part, iter_part))  20.1 us
    all_gather x1, blocking collectives, body(): lax.all_gather(h_rows, 'col', axis=1, tiled=True)  16.9 us
    dot_general x16, matrix products, add_piece(): jnp.einsum('awv,awkm->avkm', paired.astype(jnp.bfloat16), picked, preferr...  16.7 us
  transfers between devices with their start and end apart: 3, of which 1 were waited for; matrix products, arithmetic and copies ran while one was open for 0% of the time, Pallas kernels for 0%

profile of v1, /device:TPU:1, one launch (start us, length us, event | category | flops | bytes accessed | tf_op | source)
XLA Modules:
  0.0 732.6 jit_solution(10654890038585790089)
XLA Ops:
  6.5 6.4 stack.2
  13.0 15.9 %all-to-all-start = ((bf16[16,1,1,1,8,2,128,128]{7,6,5,4,3,2,1,0:T(8,128)(2,1)}), bf16[16,1,1,1,8,2,128,128]{7,6,5,4,3,2,1,0:T(8,128)(2,1)}, u32[]{:S(2)}, u32[]{:S(2)}) async-start(bf16[16,1,1,1,8,2,128,128]{7,6,5,4,3,2,1,0:T(8,128)(2,1)} %stack.2), calls=%async_computation | async-start | bytes 16777216 | tf_op jit(solution)/shard_map/all_to_all | solution.py:10
  29.7 7.3 %all_gather.27 = s32[1,4,1,8,2]{3,4,2,0,1:T(2,128)S(1)} all-gather(s32[1,1,1,8,2]{3,4,2,0,1:T(2,128)S(1)} %bitcast.96), channel_id=1, replica_groups=mesh['row'=16,'col'=8,'depth'=4] {'depth'}, dimensions={1}, use_global_device_ids=true | all-gather | bytes 320 | tf_op jit(solution)/shard_map/all_gather | solution.py:53
  37.2 6.6 all_gather.29
  43.8 16.9 %all_gather.24 = s32[1,16,1,12]{3,2,0,1:T(1,128)S(1)} all-gather(s32[1,2,1,12]{3,2,0,1:T(1,128)S(1)} %bitcast.97), channel_id=1, replica_groups=mesh['row'=16,'col'=8,'depth'=4] {'col'}, dimensions={1}, use_global_device_ids=true | all-gather | bytes 864 | tf_op jit(solution)/shard_map/all_gather | solution.py:65
  60.7 13.2 %all_gather.26 = s32[1,16,1,12]{3,2,0,1:T(1,128)S(1)} all-gather(s32[1,2,1,12]{3,2,0,1:T(1,128)S(1)} %bitcast.98), channel_id=1, replica_groups=mesh['row'=16,'col'=8,'depth'=4] {'col'}, dimensions={1}, use_global_device_ids=true | all-gather | bytes 864 | tf_op jit(solution)/shard_map/all_gather | solution.py:66
  73.9 14.7 %all_gather.30 = s32[1,16,1,12]{3,2,0,1:T(1,128)S(1)} all-gather(s32[1,2,1,12]{3,2,0,1:T(1,128)S(1)} %bitcast.99), channel_id=1, replica_groups=mesh['row'=16,'col'=8,'depth'=4] {'col'}, dimensions={1}, use_global_device_ids=true | all-gather | bytes 864 | tf_op jit(solution)/shard_map/all_gather | solution.py:67
  88.6 320.1 %all_gather.25 = s32[16,1,1,8,2]{3,4,2,1,0:T(2,128)S(1)} all-gather(s32[1,1,1,8,2]{3,4,2,1,0:T(2,128)S(1)} %copy-done.2), channel_id=1, replica_groups=mesh['row'=16,'col'=8,'depth'=4] {'row'}, dimensions={0}, use_global_device_ids=true | all-gather | bytes 1088 | tf_op jit(solution)/shard_map/all_gather | solution.py:72
  408.7 20.4 %all_gather.28 = s32[16,1,1,8,2]{3,4,2,1,0:T(2,128)S(1)} all-gather(s32[1,1,1,8,2]{3,4,2,1,0:T(2,128)S(1)} %copy-done.1), channel_id=1, replica_groups=mesh['row'=16,'col'=8,'depth'=4] {'row'}, dimensions={0}, use_global_device_ids=true | all-gather | bytes 1088 | tf_op jit(solution)/shard_map/all_gather | solution.py:73
  429.1 2.5 broadcast_in_dim.36
  431.6 222.6 %while.10 = (s32[]{:T(128)}, f32[64,128,128]{2,1,0:T(8,128)}, s32[16,12]{1,0:T(8,128)S(1)}, s32[16,8,2]{1,2,0:T(2,128)S(1)}, s32[16,12]{1,0:T(8,128)S(1)}, /*ind...) while((s32[]{:T(128)}, f32[64,128,128]{2,1,0:T(8,128)}, ...), condition=%wide.region_2.5_spmd, body=%wide.region_0.4_spmd.sunk | while | flops 103419520 | bytes 16400633 | solution.py:47
  433.1 1.1 dynamic-slice_bitcast_fusion.2
  437.4 1.4 fusion.34
  439.4 5.9 scatter_fusion
  446.9 1.1 dynamic-slice_bitcast_fusion.2
  451.2 1.4 fusion.34
  453.3 6.0 scatter_fusion
  460.8 1.1 dynamic-slice_bitcast_fusion.2
  465.1 1.4 fusion.34
  467.2 6.1 scatter_fusion
  474.8 1.1 dynamic-slice_bitcast_fusion.2
  479.1 1.4 fusion.34
  481.1 6.1 scatter_fusion
  488.8 1.1 dynamic-slice_bitcast_fusion.2
  493.0 1.4 fusion.34
  495.1 6.1 scatter_fusion
  502.7 1.1 dynamic-slice_bitcast_fusion.2
  507.0 1.4 fusion.34
  509.1 6.1 scatter_fusion
  516.6 1.1 dynamic-slice_bitcast_fusion.2
  520.9 1.4 fusion.34
  523.0 6.0 scatter_fusion
  530.5 1.1 dynamic-slice_bitcast_fusion.2
  534.8 1.4 fusion.34
  536.9 6.0 scatter_fusion
  544.4 1.1 dynamic-slice_bitcast_fusion.2
  547.7 1.0 convolution_convert_fusion.2
  548.7 1.4 fusion.34
  550.8 6.0 scatter_fusion
  558.3 1.1 dynamic-slice_bitcast_fusion.2
  562.6 1.4 fusion.34
  564.7 6.0 scatter_fusion
  572.2 1.1 dynamic-slice_bitcast_fusion.2
  576.5 1.4 fusion.34
  578.5 6.0 scatter_fusion
  586.1 1.1 dynamic-slice_bitcast_fusion.2
  590.4 1.4 fusion.34
  592.4 6.0 scatter_fusion
  600.0 1.1 dynamic-slice_bitcast_fusion.2
  604.3 1.4 fusion.34
  606.4 6.0 scatter_fusion
  613.9 1.1 dynamic-slice_bitcast_fusion.2
  618.2 1.4 fusion.34
  620.2 6.0 scatter_fusion
  627.8 1.1 dynamic-slice_bitcast_fusion.2
  631.0 1.0 convolution_convert_fusion.2
  632.1 1.4 fusion.34
  634.2 6.1 scatter_fusion
  641.8 1.1 dynamic-slice_bitcast_fusion.2
  646.0 1.4 fusion.34
  648.1 6.0 scatter_fusion
  654.1 4.0 convert_element_type.33
  658.2 65.5 %reduce-scatter.2.cloned.1.call-done = bf16[1,8,2,128,128]{4,3,2,1,0:T(8,128)(2,1)} async-done(((bf16[4,8,2,128,128]{4,3,2,1,0:T(8,128)(2,1)}), bf16[1,8,2,128,128]{4,3,2,1,0:T(8,128)(2,1)}) %reduce-scatter.2.cloned.1.call-update) | async-done | bytes 524304 | tf_op jit(solution)/shard_map/reduce_scatter | solution.py:82
  723.7 2.1 fusion.20
  (420 shorter events, 83.2 us)
Async XLA Ops:
  13.0 16.8 %copy-start.2 = (s32[1,1,1,8,2]{3,4,2,1,0:T(2,128)S(1)}, s32[1,1,1,8,2]{3,4,2,1,0:T(2,128)}, u32[]{:S(2)}) copy-start(s32[1,1,1,8,2]{3,4,2,1,0:T(2,128)} %param.19) | copy-start | bytes 196
  13.0 24.2 %copy-start.1 = (s32[1,1,1,8,2]{3,4,2,1,0:T(2,128)S(1)}, s32[1,1,1,8,2]{3,4,2,1,0:T(2,128)}, u32[]{:S(2)}) copy-start(s32[1,1,1,8,2]{3,4,2,1,0:T(2,128)} %param.20) | copy-start | bytes 196
  13.0 30.9 %copy-start.3 = (s32[1,2,1,12]{3,2,1,0:T(1,128)S(1)}, s32[1,2,1,12]{3,2,1,0:T(1,128)}, u32[]{:S(2)}) copy-start(s32[1,2,1,12]{3,2,1,0:T(1,128)} %param.15) | copy-start | bytes 292
  13.0 47.7 %copy-start.4 = (s32[1,2,1,12]{3,2,1,0:T(1,128)S(1)}, s32[1,2,1,12]{3,2,1,0:T(1,128)}, u32[]{:S(2)}) copy-start(s32[1,2,1,12]{3,2,1,0:T(1,128)} %param.16) | copy-start | bytes 292
  13.0 60.9 %copy-start.5 = (s32[1,2,1,12]{3,2,1,0:T(1,128)S(1)}, s32[1,2,1,12]{3,2,1,0:T(1,128)}, u32[]{:S(2)}) copy-start(s32[1,2,1,12]{3,2,1,0:T(1,128)} %param.17) | copy-start | bytes 292
  13.0 416.1 %all-to-all-start = ((bf16[16,1,1,1,8,2,128,128]{7,6,5,4,3,2,1,0:T(8,128)(2,1)}), bf16[16,1,1,1,8,2,128,128]{7,6,5,4,3,2,1,0:T(8,128)(2,1)}, u32[]{:S(2)}, u32[]{:S(2)}) async-start(bf16[16,1,1,1,8,2,128,128]{7,6,5,4,3,2,1,0:T(8,128)(2,1)} %stack.2), calls=%async_computation | async-start | bytes 16777216 | tf_op jit(solution)/shard_map/all_to_all | solution.py:10
  28.9 400.2 %all-gather.2.cloned.1.call-start = ((), (), s32[]{:S(2)}) async-start(), calls=%async_computation.2 | async-start | bytes 7077888 | tf_op jit(solution)/shard_map/all_gather | solution.py:64
  29.7 694.1 %reduce-scatter.2.cloned.1.call-start = ((), (), s32[]{:S(2)}) async-start(), calls=%async_computation.3 | async-start | bytes 2621440 | tf_op jit(solution)/shard_map/reduce_scatter | solution.py:82
  654.1 69.6 %copy-start = (bf16[1,1,1,8,2,128,128]{6,5,4,3,2,1,0:T(8,128)(2,1)S(1)}, bf16[1,1,1,8,2,128,128]{6,5,4,3,2,1,0:T(8,128)(2,1)}, u32[]{:S(2)}) copy-start(bf16[1,1,1,8,2,128,128]{6,5,4,3,2,1,0:T(8,128)(2,1)} %param.21) | copy-start | bytes 1572868
Sparse Core Ops, SparseCore 0:
  31.8 81.7 all-gather.1
  658.2 65.4 reduce-scatter.1
